TPU v7x, 256 devices: a whole 4x4x8 slice. The times are simulated.
256 devices in a mesh: leaf: 32 (over z, y), front: 8 (over x, core).
Axes of the slice: x: 4, y: 4, z: 8, core: 2. Of those that a mesh axis runs over, the one named last changes fastest.
Arguments:
- section_updates: bfloat16 [32768, 256], P(('leaf', 'front')), may hold values from -6 to 6
- upper_rhs: float32 [126976, 256], P(('leaf', 'front')), may hold values from -6 to 6
- pivot_inverse: bfloat16 [126976, 4096], P('leaf', 'front'), may hold values from -0.09375 to 0.09375
- coupling: bfloat16 [1024, 122880], P('front', 'leaf'), may hold values from -0.09375 to 0.09375
- extend_lists: int32 [62, 8], replicated, may hold values from 0 to 39, as said below
Outputs:
- solution: float32 [126976, 256], P(('leaf', 'front'))
- interface: bfloat16 [32768, 256], P(('leaf', 'front'))
Inputs may be any that keep to these rules, and one draw needn't show every extreme that they name: `extend_lists`: each row names 8 different blocks of the parent's frame; the rows of the root's two children name pivot blocks only, below 32.
All inputs are finite; a program needn't handle non-finite values.
Results may differ from a plain program's by a relative error of at most 0.022.
Values may be sent and summed in bfloat16 or wider, within the bound.
A program may use at most 64 MiB of HBM per device.

v0:
```python
import jax
import jax.numpy as jnp
from jax import lax
from jax.sharding import PartitionSpec as P

PIV = 4096
UPD = 1024
BLK = 128


def partner(block, axis, stride):
    count = lax.axis_size(axis)
    route = []
    for low in range(count):
        high = low | 1 << stride
        if high != low and high < count:
            route += [(low, high), (high, low)]
    return lax.ppermute(block, axis, route)


def child_base(leaves, height):
    total_rows = 0
    for depth in range(height - 1):
        total_rows = total_rows + leaves // 2**depth
    return total_rows


def list_row(extend_lists, row_index):
    return lax.dynamic_slice_in_dim(extend_lists, row_index, 1, 0)[0]


def upper_bit(position, bit_index):
    return position >> bit_index & 1 == 1


def joined(position, bit_index, portion, partner_rows):
    return jnp.where(
        upper_bit(position, bit_index),
        jnp.concatenate([partner_rows, portion], 0),
        jnp.concatenate([portion, partner_rows], 0),
    )


def gather_own(portion, height, position):
    for bit_index in range(height):
        partner_rows = partner(portion.astype(jnp.bfloat16), "leaf", bit_index).astype(
            portion.dtype
        )
        portion = joined(position, bit_index, portion, partner_rows)
    return portion


def sum_updates(summand, height):
    for bit_index in range(height):
        summand = summand + partner(summand.astype(jnp.bfloat16), "leaf", bit_index).astype(
            summand.dtype
        )
    return summand


def sum_solution(summand, height):
    for bit_index in range(height):
        summand = summand + partner(summand.astype(jnp.bfloat16), "leaf", bit_index).astype(
            summand.dtype
        )
    return summand


def front_sum(summand):
    bits = lax.axis_size("front").bit_length() - 1
    for bit_index in range(bits):
        half = summand.astype(jnp.bfloat16)
        summand = half.astype(jnp.float32) + partner(half, "front", bit_index).astype(jnp.float32)
    return summand


def per_device(section_updates, upper_rhs, pivot_inverse, coupling, extend_lists):
    leaves = lax.axis_size("leaf")
    fronts = lax.axis_size("front")
    levels = leaves.bit_length() - 1
    position = lax.axis_index("leaf")
    column = lax.axis_index("front")
    rhs_width = upper_rhs.shape[1]
    piv_dev = PIV // fronts
    upd_dev = UPD // fronts
    piv_blocks = piv_dev // BLK
    upd_blocks = upd_dev // BLK
    block_count = UPD // BLK
    local_blocks = jnp.concatenate(
        [
            column * piv_blocks + jnp.arange(piv_blocks, dtype=jnp.int32),
            PIV // BLK + column * upd_blocks + jnp.arange(upd_blocks, dtype=jnp.int32),
        ]
    )
    local_count = piv_blocks + upd_blocks
    carried = section_updates
    saved_part = []
    saved_half = []
    for height in range(1, levels + 1):
        group_size = 2**height
        span_rows = PIV // group_size
        band_start = PIV - PIV // 2 ** (height - 1)
        rhs_len = piv_dev // group_size
        rhs_start = piv_dev - piv_dev // 2 ** (height - 1)
        member = position & group_size - 1
        own_child = child_base(leaves, height) + (position >> height - 1)
        sibling = partner(carried, "leaf", height - 1)
        pair_blocks = lax.all_gather(jnp.stack([carried, sibling]), "front", axis=1, tiled=True)
        pair_lists = jnp.stack(
            [list_row(extend_lists, own_child), list_row(extend_lists, own_child ^ 1)]
        )
        chooser = (pair_lists.reshape(2 * block_count)[None, :] == local_blocks[:, None]).astype(
            jnp.bfloat16
        )
        assembled = jnp.dot(
            chooser,
            pair_blocks.reshape(2 * block_count, BLK * rhs_width),
            preferred_element_type=jnp.float32,
        ).reshape(local_count * BLK, rhs_width)
        own_rows = gather_own(upper_rhs[rhs_start : rhs_start + rhs_len], height, position)
        rows_half = (own_rows + assembled[:piv_dev]).astype(jnp.bfloat16)
        g_share = pivot_inverse[band_start : band_start + span_rows]
        pivot_part = front_sum(jnp.dot(g_share, rows_half, preferred_element_type=jnp.float32))
        pivot_half = pivot_part.astype(jnp.bfloat16)
        saved_part.append(pivot_part)
        saved_half.append(pivot_half)
        if height < levels:
            c_share = coupling[:, band_start : band_start + span_rows]
            summand = jnp.dot(c_share, pivot_half, preferred_element_type=jnp.float32)
            frame_upd = assembled[piv_dev:]
            carried = (frame_upd - sum_updates(summand, height)).astype(jnp.bfloat16)
    from_above = carried
    outputs = []
    for height in range(levels, 0, -1):
        group_size = 2**height
        span_rows = PIV // group_size
        band_start = PIV - PIV // 2 ** (height - 1)
        member = position & group_size - 1
        pivot_part = saved_part[height - 1]
        if height < levels:
            c_share = coupling[:, band_start : band_start + span_rows]
            back_total = front_sum(
                jnp.einsum("up,ur->pr", c_share, from_above, preferred_element_type=jnp.float32)
            )
            weight_half = (pivot_part - back_total).astype(jnp.bfloat16)
            upper_rows = from_above
        else:
            weight_half = saved_half[height - 1]
            upper_rows = jnp.zeros((upd_dev, rhs_width), jnp.bfloat16)
        g_share = pivot_inverse[band_start : band_start + span_rows]
        solve_term = jnp.einsum(
            "cp,cr->pr", g_share, weight_half, preferred_element_type=jnp.float32
        )
        part_len = piv_dev // group_size
        summed = sum_solution(solve_term, height)
        portion = lax.dynamic_slice_in_dim(summed, member * part_len, part_len, 0)
        rows_half = summed.astype(jnp.bfloat16)
        outputs.append(portion)
        frame_half = jnp.concatenate([rows_half, upper_rows], 0).reshape(
            local_count, BLK * rhs_width
        )
        child_list = list_row(extend_lists, child_base(leaves, height) + (position >> height - 1))
        picker = (child_list[:, None] == local_blocks[None, :]).astype(jnp.bfloat16)
        outgoing = (
            jnp.dot(picker, frame_half, preferred_element_type=jnp.float32)
            .astype(jnp.bfloat16)
            .reshape(fronts, upd_dev, rhs_width)
        )
        incoming = lax.all_to_all(outgoing, "front", split_axis=0, concat_axis=0, tiled=True)
        from_above = jnp.sum(incoming, axis=0, dtype=jnp.float32).astype(jnp.bfloat16)
    solution = jnp.concatenate(outputs[::-1], 0)
    return (solution, from_above)


def solution(mesh):
    placed = (
        P(("leaf", "front"), None),
        P(("leaf", "front"), None),
        P("leaf", "front"),
        P("front", "leaf"),
        P(),
    )
    return jax.shard_map(
        per_device,
        mesh=mesh,
        in_specs=placed,
        out_specs=(P(("leaf", "front"), None), P(("leaf", "front"), None)),
        check_vma=False,
    )
```

profile of v0, /device:TPU:24, one launch (start us, length us, event | category | flops | bytes accessed | tf_op | source)
XLA Modules:
  0.0 750.2 jit_solution(16977858934660072619)
XLA Ops:
  20.1 21.8 %all-gather.6.cloned.1.call-done = bf16[2,1024,256]{2,1,0:T(8,128)(2,1)} async-done(((bf16[2,128,256]{2,1,0:T(8,128)(2,1)}), bf16[2,1024,256]{2,1,0:T(8,128)(2,1)}) %all-gather.6.cloned.1.call-update) | async-done | bytes 1048592 | tf_op jit(solution)/shard_map/all_gather | solution.py:108
  50.2 25.3 %collective-permute-done.3 = bf16[2048,256]{0,1:T(8,128)(2,1)S(1)} collective-permute-done((bf16[2048,256]{0,1:T(8,128)(2,1)S(1)}, bf16[2048,256]{0,1:T(8,128)(2,1)S(1)}, u32[]{:S(2)}, u32[]{:S(2)}) %collective-permute-start.3) | collective-permute-done | bytes 1048608 | tf_op jit(solution)/shard_map/ppermute | solution.py:18
  77.7 24.3 %collective-permute-done.4 = bf16[2048,256]{0,1:T(8,128)(2,1)S(1)} collective-permute-done((bf16[2048,256]{0,1:T(8,128)(2,1)S(1)}, bf16[2048,256]{0,1:T(8,128)(2,1)S(1)}, u32[]{:S(2)}, u32[]{:S(2)}) %collective-permute-start.4) | collective-permute-done | bytes 1048608 | tf_op jit(solution)/shard_map/ppermute | solution.py:18
  108.8 5.4 collective-permute-done.8
  120.6 5.9 collective-permute-done.6
  126.5 13.9 %all-gather.8.cloned.1.call-done = bf16[2,1024,256]{1,2,0:T(8,128)(2,1)} async-done(((bf16[2,128,256]{1,2,0:T(8,128)(2,1)}), bf16[2,1024,256]{1,2,0:T(8,128)(2,1)}) %all-gather.8.cloned.1.call-update) | async-done | bytes 1048592 | tf_op jit(solution)/shard_map/all_gather | solution.py:108
  148.6 13.1 %collective-permute-done.10 = bf16[1024,256]{0,1:T(8,128)(2,1)S(1)} collective-permute-done((bf16[1024,256]{0,1:T(8,128)(2,1)S(1)}, bf16[1024,256]{0,1:T(8,128)(2,1)S(1)}, u32[]{:S(2)}, u32[]{:S(2)}) %collective-permute-start.10) | collective-permute-done | bytes 524320 | tf_op jit(solution)/shard_map/ppermute | solution.py:18
  164.7 12.0 %collective-permute-done.11 = bf16[1024,256]{0,1:T(8,128)(2,1)S(1)} collective-permute-done((bf16[1024,256]{0,1:T(8,128)(2,1)S(1)}, bf16[1024,256]{0,1:T(8,128)(2,1)S(1)}, u32[]{:S(2)}, u32[]{:S(2)}) %collective-permute-start.11) | collective-permute-done | bytes 524320 | tf_op jit(solution)/shard_map/ppermute | solution.py:18
  199.8 5.0 collective-permute-done.13
  210.5 11.0 %all-gather.10.cloned.1.call-done = bf16[2,1024,256]{1,2,0:T(8,128)(2,1)} async-done(((bf16[2,128,256]{1,2,0:T(8,128)(2,1)}), bf16[2,1024,256]{1,2,0:T(8,128)(2,1)}) %all-gather.10.cloned.1.call-update) | async-done | bytes 1048592 | tf_op jit(solution)/shard_map/all_gather | solution.py:108
  231.5 7.5 %collective-permute-done.19 = bf16[512,256]{0,1:T(8,128)(2,1)S(1)} collective-permute-done((bf16[512,256]{0,1:T(8,128)(2,1)S(1)}, bf16[512,256]{0,1:T(8,128)(2,1)S(1)}, u32[]{:S(2)}, u32[]{:S(2)}) %collective-permute-start.19) | collective-permute-done | bytes 262176 | tf_op jit(solution)/shard_map/ppermute | solution.py:18
  241.9 6.4 collective-permute-done.20
  255.4 5.0 collective-permute-done.26
  295.3 4.6 all-gather.12.cloned.1.call-done
  309.6 4.7 collective-permute-done.30
  327.9 4.9 collective-permute-done.38
  345.5 6.5 collective-permute-start.41
  358.9 5.2 collective-permute-done.33
  374.1 6.8 collective-permute-start.36
  403.3 6.7 collective-permute-done.45
  410.4 7.6 %collective-permute-done.46 = bf16[512,256]{0,1:T(8,128)(2,1)S(1)} collective-permute-done((bf16[512,256]{0,1:T(8,128)(2,1)S(1)}, bf16[512,256]{0,1:T(8,128)(2,1)S(1)}, u32[]{:S(2)}, u32[]{:S(2)}) %collective-permute-start.46) | collective-permute-done | bytes 262176 | tf_op jit(solution)/shard_map/ppermute | solution.py:18
  419.6 6.9 collective-permute-done.47
  429.0 13.4 %collective-permute-done.48 = bf16[512,256]{0,1:T(8,128)(2,1)S(1)} collective-permute-done((bf16[512,256]{0,1:T(8,128)(2,1)S(1)}, bf16[512,256]{0,1:T(8,128)(2,1)S(1)}, u32[]{:S(2)}, u32[]{:S(2)}) %collective-permute-start.48) | collective-permute-done | bytes 262176 | tf_op jit(solution)/shard_map/ppermute | solution.py:18
  442.5 5.4 collective-permute-start.49
  447.9 7.8 %collective-permute-done.49 = bf16[512,256]{0,1:T(8,128)(2,1)S(1)} collective-permute-done((bf16[512,256]{0,1:T(8,128)(2,1)S(1)}, bf16[512,256]{0,1:T(8,128)(2,1)S(1)}, u32[]{:S(2)}, u32[]{:S(2)}) %collective-permute-start.49) | collective-permute-done | bytes 262176 | tf_op jit(solution)/shard_map/ppermute | solution.py:18
  457.6 14.1 %all_to_all.25 = bf16[8,128,256]{2,1,0:T(8,128)(2,1)S(1)} all-to-all(bf16[8,128,256]{2,1,0:T(8,128)(2,1)S(1)} %copy.50), channel_id=1, replica_groups=mesh['leaf'=32,'front'=8] {'front'}, dimensions={0} | all-to-all | bytes 1048576 | tf_op jit(solution)/shard_map/all_to_all | solution.py:169
  474.1 5.0 collective-permute-done.51
  480.1 5.6 collective-permute-done.52
  487.7 7.0 collective-permute-done.53
  494.9 7.9 %collective-permute-done.54 = bf16[512,256]{0,1:T(8,128)(2,1)S(1)} collective-permute-done((bf16[512,256]{0,1:T(8,128)(2,1)S(1)}, bf16[512,256]{0,1:T(8,128)(2,1)S(1)}, u32[]{:S(2)}, u32[]{:S(2)}) %collective-permute-start.54) | collective-permute-done | bytes 262176 | tf_op jit(solution)/shard_map/ppermute | solution.py:18
  503.0 8.5 %collective-permute-done.55 = bf16[512,256]{0,1:T(8,128)(2,1)S(1)} collective-permute-done((bf16[512,256]{0,1:T(8,128)(2,1)S(1)}, bf16[512,256]{0,1:T(8,128)(2,1)S(1)}, u32[]{:S(2)}, u32[]{:S(2)}) %collective-permute-start.55) | collective-permute-done | bytes 262176 | tf_op jit(solution)/shard_map/ppermute | solution.py:18
  514.1 7.6 %collective-permute-done.56 = bf16[512,256]{0,1:T(8,128)(2,1)} collective-permute-done((bf16[512,256]{0,1:T(8,128)(2,1)}, bf16[512,256]{0,1:T(8,128)(2,1)}, u32[]{:S(2)}, u32[]{:S(2)}) %collective-permute-start.56) | collective-permute-done | bytes 262176 | tf_op jit(solution)/shard_map/ppermute | solution.py:18
  524.9 13.6 %all_to_all.26 = bf16[8,128,256]{2,1,0:T(8,128)(2,1)} all-to-all(bf16[8,128,256]{2,1,0:T(8,128)(2,1)S(1)} %copy.54), channel_id=1, replica_groups=mesh['leaf'=32,'front'=8] {'front'}, dimensions={0} | all-to-all | bytes 1048576 | tf_op jit(solution)/shard_map/all_to_all | solution.py:169
  542.2 7.8 %collective-permute-done.58 = bf16[512,256]{0,1:T(8,128)(2,1)S(1)} collective-permute-done((bf16[512,256]{0,1:T(8,128)(2,1)S(1)}, bf16[512,256]{0,1:T(8,128)(2,1)S(1)}, u32[]{:S(2)}, u32[]{:S(2)}) %collective-permute-start.58) | collective-permute-done | bytes 262176 | tf_op jit(solution)/shard_map/ppermute | solution.py:18
  551.0 8.1 %collective-permute-done.59 = bf16[512,256]{0,1:T(8,128)(2,1)S(1)} collective-permute-done((bf16[512,256]{0,1:T(8,128)(2,1)S(1)}, bf16[512,256]{0,1:T(8,128)(2,1)S(1)}, u32[]{:S(2)}, u32[]{:S(2)}) %collective-permute-start.59) | collective-permute-done | bytes 262176 | tf_op jit(solution)/shard_map/ppermute | solution.py:18
  560.7 7.5 collective-permute-done.60
  568.3 7.9 %collective-permute-done.61 = bf16[512,256]{0,1:T(8,128)(2,1)S(1)} collective-permute-done((bf16[512,256]{0,1:T(8,128)(2,1)S(1)}, bf16[512,256]{0,1:T(8,128)(2,1)S(1)}, u32[]{:S(2)}, u32[]{:S(2)}) %collective-permute-start.61) | collective-permute-done | bytes 262176 | tf_op jit(solution)/shard_map/ppermute | solution.py:18
  577.8 6.6 collective-permute-done.62
  587.4 12.8 %all_to_all.27 = bf16[8,128,256]{2,1,0:T(8,128)(2,1)S(1)} all-to-all(bf16[8,128,256]{2,1,0:T(8,128)(2,1)S(1)} %copy.58), channel_id=1, replica_groups=mesh['leaf'=32,'front'=8] {'front'}, dimensions={0} | all-to-all | bytes 1048576 | tf_op jit(solution)/shard_map/all_to_all | solution.py:169
  603.4 13.4 %collective-permute-done.64 = bf16[1024,256]{0,1:T(8,128)(2,1)S(1)} collective-permute-done((bf16[1024,256]{0,1:T(8,128)(2,1)S(1)}, bf16[1024,256]{0,1:T(8,128)(2,1)S(1)}, u32[]{:S(2)}, u32[]{:S(2)}) %collective-permute-start.64) | collective-permute-done | bytes 524320 | tf_op jit(solution)/shard_map/ppermute | solution.py:18
  618.0 13.7 %collective-permute-done.65 = bf16[1024,256]{0,1:T(8,128)(2,1)S(1)} collective-permute-done((bf16[1024,256]{0,1:T(8,128)(2,1)S(1)}, bf16[1024,256]{0,1:T(8,128)(2,1)S(1)}, u32[]{:S(2)}, u32[]{:S(2)}) %collective-permute-start.65) | collective-permute-done | bytes 524320 | tf_op jit(solution)/shard_map/ppermute | solution.py:18
  633.5 7.5 collective-permute-done.66
  641.3 7.7 %collective-permute-done.67 = bf16[512,256]{0,1:T(8,128)(2,1)S(1)} collective-permute-done((bf16[512,256]{0,1:T(8,128)(2,1)S(1)}, bf16[512,256]{0,1:T(8,128)(2,1)S(1)}, u32[]{:S(2)}, u32[]{:S(2)}) %collective-permute-start.67) | collective-permute-done | bytes 262176 | tf_op jit(solution)/shard_map/ppermute | solution.py:18
  651.0 13.0 %all_to_all.28 = bf16[8,128,256]{2,1,0:T(8,128)(2,1)S(1)} all-to-all(bf16[8,128,256]{2,1,0:T(8,128)(2,1)S(1)} %copy.62), channel_id=1, replica_groups=mesh['leaf'=32,'front'=8] {'front'}, dimensions={0} | all-to-all | bytes 1048576 | tf_op jit(solution)/shard_map/all_to_all | solution.py:169
  668.3 24.6 %collective-permute-done.69 = bf16[2048,256]{0,1:T(8,128)(2,1)S(1)} collective-permute-done((bf16[2048,256]{0,1:T(8,128)(2,1)S(1)}, bf16[2048,256]{0,1:T(8,128)(2,1)S(1)}, u32[]{:S(2)}, u32[]{:S(2)}) %collective-permute-start.69) | collective-permute-done | bytes 1048608 | tf_op jit(solution)/shard_map/ppermute | solution.py:18
  694.3 25.0 %collective-permute-done.70 = bf16[2048,256]{0,1:T(8,128)(2,1)S(1)} collective-permute-done((bf16[2048,256]{0,1:T(8,128)(2,1)S(1)}, bf16[2048,256]{0,1:T(8,128)(2,1)S(1)}, u32[]{:S(2)}, u32[]{:S(2)}) %collective-permute-start.70) | collective-permute-done | bytes 1048608 | tf_op jit(solution)/shard_map/ppermute | solution.py:18
  721.3 5.5 collective-permute-done.71
  736.4 6.1 all-to-all-done.4
  (374 shorter events, 261.2 us)
Async XLA Ops:
  7.2 34.8 %all-gather.6.cloned.1.call-start = ((), (), s32[]{:S(2)}) async-start(), calls=%async_computation.5 | async-start | bytes 1179648 | tf_op jit(solution)/shard_map/all_gather | solution.py:108
  13.3 127.1 %all-gather.8.cloned.1.call-start = ((), (), s32[]{:S(2)}) async-start(), calls=%async_computation.6 | async-start | bytes 1179648 | tf_op jit(solution)/shard_map/all_gather | solution.py:108
  50.1 25.4 %collective-permute-start.3 = (bf16[2048,256]{0,1:T(8,128)(2,1)S(1)}, bf16[2048,256]{0,1:T(8,128)(2,1)S(1)}, u32[]{:S(2)}, u32[]{:S(2)}) collective-permute-start(bf16[2048,256]{0,1:T(8,128)(2,1)S(1)} %add_convert_fusion.3), channel_id=1, source_target_pairs={{0,2},{2,0},{1,3},{3,1},{4,6},{6,4},{5,7},{7,5},{8,10},{10,8},{9,1... | collective-permute-start | bytes 3145736 | tf_op jit(solution)/shard_map/ppermute | solution.py:18
  76.0 26.0 %collective-permute-start.4 = (bf16[2048,256]{0,1:T(8,128)(2,1)S(1)}, bf16[2048,256]{0,1:T(8,128)(2,1)S(1)}, u32[]{:S(2)}, u32[]{:S(2)}) collective-permute-start(bf16[2048,256]{0,1:T(8,128)(2,1)S(1)} %add_convert_fusion.2), channel_id=1, source_target_pairs={{0,4},{4,0},{1,5},{5,1},{2,6},{6,2},{3,7},{7,3},{8,12},{12,8},{9,1... | collective-permute-start | bytes 3145736 | tf_op jit(solution)/shard_map/ppermute | solution.py:18
  107.9 6.3 collective-permute-start.8
  114.9 106.6 %all-gather.10.cloned.1.call-start = ((), (), s32[]{:S(2)}) async-start(), calls=%async_computation.7 | async-start | bytes 1179648 | tf_op jit(solution)/shard_map/all_gather | solution.py:108
  120.0 6.5 collective-permute-start.6
  147.4 14.4 %collective-permute-start.10 = (bf16[1024,256]{0,1:T(8,128)(2,1)S(1)}, bf16[1024,256]{0,1:T(8,128)(2,1)S(1)}, u32[]{:S(2)}, u32[]{:S(2)}) collective-permute-start(bf16[1024,256]{0,1:T(8,128)(2,1)S(1)} %add_convert_fusion.7), channel_id=1, source_target_pairs={{0,2},{2,0},{1,3},{3,1},{4,6},{6,4},{5,7},{7,5},{8,10},{10,8},{9,1... | collective-permute-start | bytes 1572872 | tf_op jit(solution)/shard_map/ppermute | solution.py:18
  162.0 14.8 %collective-permute-start.11 = (bf16[1024,256]{0,1:T(8,128)(2,1)S(1)}, bf16[1024,256]{0,1:T(8,128)(2,1)S(1)}, u32[]{:S(2)}, u32[]{:S(2)}) collective-permute-start(bf16[1024,256]{0,1:T(8,128)(2,1)S(1)} %add_convert_fusion.6), channel_id=1, source_target_pairs={{0,4},{4,0},{1,5},{5,1},{2,6},{6,2},{3,7},{7,3},{8,12},{12,8},{9,1... | collective-permute-start | bytes 1572872 | tf_op jit(solution)/shard_map/ppermute | solution.py:18
  183.8 5.9 collective-permute-start.16
  194.8 105.1 %all-gather.12.cloned.1.call-start = ((), (), s32[]{:S(2)}) async-start(), calls=%async_computation.8 | async-start | bytes 1179648 | tf_op jit(solution)/shard_map/all_gather | solution.py:108
  198.9 5.9 collective-permute-start.13
  230.5 8.5 %collective-permute-start.19 = (bf16[512,256]{0,1:T(8,128)(2,1)S(1)}, bf16[512,256]{0,1:T(8,128)(2,1)S(1)}, u32[]{:S(2)}, u32[]{:S(2)}) collective-permute-start(bf16[512,256]{0,1:T(8,128)(2,1)S(1)} %add_convert_fusion.11), channel_id=1, source_target_pairs={{0,2},{2,0},{1,3},{3,1},{4,6},{6,4},{5,7},{7,5},{8,10},{10,8},{9,1... | collective-permute-start | bytes 786440 | tf_op jit(solution)/shard_map/ppermute | solution.py:18
  239.1 9.2 %collective-permute-start.20 = (bf16[512,256]{0,1:T(8,128)(2,1)S(1)}, bf16[512,256]{0,1:T(8,128)(2,1)S(1)}, u32[]{:S(2)}, u32[]{:S(2)}) collective-permute-start(bf16[512,256]{0,1:T(8,128)(2,1)S(1)} %add_convert_fusion.10), channel_id=1, source_target_pairs={{0,4},{4,0},{1,5},{5,1},{2,6},{6,2},{3,7},{7,3},{8,12},{12,8},{9,1... | collective-permute-start | bytes 786440 | tf_op jit(solution)/shard_map/ppermute | solution.py:18
  254.5 5.9 collective-permute-start.26
  273.1 111.0 %all-gather.14.cloned.1.call-start = ((), (), s32[]{:S(2)}) async-start(), calls=%async_computation.9 | async-start | bytes 1179648 | tf_op jit(solution)/shard_map/all_gather | solution.py:108
  277.0 5.9 collective-permute-start.22
  288.0 7.3 collective-permute-start.24
  308.6 5.7 collective-permute-start.30
  314.4 6.6 collective-permute-start.31
  326.9 5.9 collective-permute-start.38
  345.5 8.7 %collective-permute-start.41 = (bf16[128,256]{0,1:T(8,128)(2,1)S(1)}, bf16[128,256]{0,1:T(8,128)(2,1)S(1)}, u32[]{:S(2)}, u32[]{:S(2)}) collective-permute-start(bf16[128,256]{0,1:T(8,128)(2,1)S(1)} %subtract_convert_fusion.8), channel_id=1, source_target_pairs={{0,128},{128,0},{8,136},{136,8},{16,144},{144,16},{24,152},{152,24... | collective-permute-start | bytes 196616 | tf_op jit(solution)/shard_map/ppermute | solution.py:18
  374.1 9.8 %collective-permute-start.36 = (bf16[256,256]{1,0:T(8,128)(2,1)S(1)}, bf16[256,256]{1,0:T(8,128)(2,1)S(1)}, u32[]{:S(2)}, u32[]{:S(2)}) collective-permute-start(bf16[256,256]{1,0:T(8,128)(2,1)S(1)} %get-tuple-element.30), channel_id=1, source_target_pairs={{0,128},{128,0},{8,136},{136,8},{16,144},{144,16},{24,152},{152,24... | collective-permute-start | bytes 393224 | tf_op jit(solution)/shard_map/ppermute | solution.py:18
  395.7 5.9 collective-permute-start.44
  402.7 7.4 collective-permute-start.45
  410.1 8.0 %collective-permute-start.46 = (bf16[512,256]{0,1:T(8,128)(2,1)S(1)}, bf16[512,256]{0,1:T(8,128)(2,1)S(1)}, u32[]{:S(2)}, u32[]{:S(2)}) collective-permute-start(bf16[512,256]{0,1:T(8,128)(2,1)S(1)} %fusion.36), channel_id=1, source_target_pairs={{0,16},{16,0},{8,24},{24,8},{32,48},{48,32},{40,56},{56,40},{64,80... | collective-permute-start | bytes 786440 | tf_op jit(solution)/shard_map/ppermute | solution.py:18
  418.2 8.3 %collective-permute-start.47 = (bf16[512,256]{0,1:T(8,128)(2,1)S(1)}, bf16[512,256]{0,1:T(8,128)(2,1)S(1)}, u32[]{:S(2)}, u32[]{:S(2)}) collective-permute-start(bf16[512,256]{0,1:T(8,128)(2,1)S(1)} %get-tuple-element.28), channel_id=1, source_target_pairs={{0,32},{32,0},{8,40},{40,8},{16,48},{48,16},{24,56},{56,24},{64,96... | collective-permute-start | bytes 786440 | tf_op jit(solution)/shard_map/ppermute | solution.py:18
  426.6 15.8 %collective-permute-start.48 = (bf16[512,256]{0,1:T(8,128)(2,1)S(1)}, bf16[512,256]{0,1:T(8,128)(2,1)S(1)}, u32[]{:S(2)}, u32[]{:S(2)}) collective-permute-start(bf16[512,256]{0,1:T(8,128)(2,1)S(1)} %fusion.37), channel_id=1, source_target_pairs={{0,64},{64,0},{8,72},{72,8},{16,80},{80,16},{24,88},{88,24},{32,96... | collective-permute-start | bytes 786440 | tf_op jit(solution)/shard_map/ppermute | solution.py:18
  442.5 13.2 %collective-permute-start.49 = (bf16[512,256]{0,1:T(8,128)(2,1)S(1)}, bf16[512,256]{0,1:T(8,128)(2,1)S(1)}, u32[]{:S(2)}, u32[]{:S(2)}) collective-permute-start(bf16[512,256]{0,1:T(8,128)(2,1)S(1)} %fusion.58), channel_id=1, source_target_pairs={{0,128},{128,0},{8,136},{136,8},{16,144},{144,16},{24,152},{152,24... | collective-permute-start | bytes 786440 | tf_op jit(solution)/shard_map/ppermute | solution.py:18
  473.5 5.6 collective-permute-start.51
  479.2 6.6 collective-permute-start.52
  487.0 7.8 %collective-permute-start.53 = (bf16[512,256]{0,1:T(8,128)(2,1)S(1)}, bf16[512,256]{0,1:T(8,128)(2,1)S(1)}, u32[]{:S(2)}, u32[]{:S(2)}) collective-permute-start(bf16[512,256]{0,1:T(8,128)(2,1)S(1)} %get-tuple-element.73), channel_id=1, source_target_pairs={{0,8},{8,0},{16,24},{24,16},{32,40},{40,32},{48,56},{56,48},{64,72... | collective-permute-start | bytes 786440 | tf_op jit(solution)/shard_map/ppermute | solution.py:18
  494.8 8.0 %collective-permute-start.54 = (bf16[512,256]{0,1:T(8,128)(2,1)S(1)}, bf16[512,256]{0,1:T(8,128)(2,1)S(1)}, u32[]{:S(2)}, u32[]{:S(2)}) collective-permute-start(bf16[512,256]{0,1:T(8,128)(2,1)S(1)} %fusion.38), channel_id=1, source_target_pairs={{0,16},{16,0},{8,24},{24,8},{32,48},{48,32},{40,56},{56,40},{64,80... | collective-permute-start | bytes 786440 | tf_op jit(solution)/shard_map/ppermute | solution.py:18
  502.9 8.6 %collective-permute-start.55 = (bf16[512,256]{0,1:T(8,128)(2,1)S(1)}, bf16[512,256]{0,1:T(8,128)(2,1)S(1)}, u32[]{:S(2)}, u32[]{:S(2)}) collective-permute-start(bf16[512,256]{0,1:T(8,128)(2,1)S(1)} %fusion.111), channel_id=1, source_target_pairs={{0,32},{32,0},{8,40},{40,8},{16,48},{48,16},{24,56},{56,24},{64,96... | collective-permute-start | bytes 786440 | tf_op jit(solution)/shard_map/ppermute | solution.py:18
  512.3 9.4 %collective-permute-start.56 = (bf16[512,256]{0,1:T(8,128)(2,1)}, bf16[512,256]{0,1:T(8,128)(2,1)}, u32[]{:S(2)}, u32[]{:S(2)}) collective-permute-start(bf16[512,256]{0,1:T(8,128)(2,1)} %fusion.39), channel_id=1, source_target_pairs={{0,64},{64,0},{8,72},{72,8},{16,80},{80,16},{24,88},{88,24},{32,96... | collective-permute-start | bytes 786440 | tf_op jit(solution)/shard_map/ppermute | solution.py:18
  541.5 8.4 %collective-permute-start.58 = (bf16[512,256]{0,1:T(8,128)(2,1)S(1)}, bf16[512,256]{0,1:T(8,128)(2,1)S(1)}, u32[]{:S(2)}, u32[]{:S(2)}) collective-permute-start(bf16[512,256]{0,1:T(8,128)(2,1)S(1)} %add_convert_fusion.9), channel_id=1, source_target_pairs={{0,2},{2,0},{1,3},{3,1},{4,6},{6,4},{5,7},{7,5},{8,10},{10,8},{9,1... | collective-permute-start | bytes 786440 | tf_op jit(solution)/shard_map/ppermute | solution.py:18
  550.0 9.1 %collective-permute-start.59 = (bf16[512,256]{0,1:T(8,128)(2,1)S(1)}, bf16[512,256]{0,1:T(8,128)(2,1)S(1)}, u32[]{:S(2)}, u32[]{:S(2)}) collective-permute-start(bf16[512,256]{0,1:T(8,128)(2,1)S(1)} %add_convert_fusion.8), channel_id=1, source_target_pairs={{0,4},{4,0},{1,5},{5,1},{2,6},{6,2},{3,7},{7,3},{8,12},{12,8},{9,1... | collective-permute-start | bytes 786440 | tf_op jit(solution)/shard_map/ppermute | solution.py:18
  560.6 7.6 %collective-permute-start.60 = (bf16[512,256]{0,1:T(8,128)(2,1)S(1)}, bf16[512,256]{0,1:T(8,128)(2,1)S(1)}, u32[]{:S(2)}, u32[]{:S(2)}) collective-permute-start(bf16[512,256]{0,1:T(8,128)(2,1)S(1)} %get-tuple-element.75), channel_id=1, source_target_pairs={{0,8},{8,0},{16,24},{24,16},{32,40},{40,32},{48,56},{56,48},{64,72... | collective-permute-start | bytes 786440 | tf_op jit(solution)/shard_map/ppermute | solution.py:18
  568.2 8.0 %collective-permute-start.61 = (bf16[512,256]{0,1:T(8,128)(2,1)S(1)}, bf16[512,256]{0,1:T(8,128)(2,1)S(1)}, u32[]{:S(2)}, u32[]{:S(2)}) collective-permute-start(bf16[512,256]{0,1:T(8,128)(2,1)S(1)} %fusion.40), channel_id=1, source_target_pairs={{0,16},{16,0},{8,24},{24,8},{32,48},{48,32},{40,56},{56,40},{64,80... | collective-permute-start | bytes 786440 | tf_op jit(solution)/shard_map/ppermute | solution.py:18
  577.7 6.7 collective-permute-start.62
  602.8 14.1 %collective-permute-start.64 = (bf16[1024,256]{0,1:T(8,128)(2,1)S(1)}, bf16[1024,256]{0,1:T(8,128)(2,1)S(1)}, u32[]{:S(2)}, u32[]{:S(2)}) collective-permute-start(bf16[1024,256]{0,1:T(8,128)(2,1)S(1)} %add_convert_fusion.5), channel_id=1, source_target_pairs={{0,2},{2,0},{1,3},{3,1},{4,6},{6,4},{5,7},{7,5},{8,10},{10,8},{9,1... | collective-permute-start | bytes 1572872 | tf_op jit(solution)/shard_map/ppermute | solution.py:18
  617.0 14.7 %collective-permute-start.65 = (bf16[1024,256]{0,1:T(8,128)(2,1)S(1)}, bf16[1024,256]{0,1:T(8,128)(2,1)S(1)}, u32[]{:S(2)}, u32[]{:S(2)}) collective-permute-start(bf16[1024,256]{0,1:T(8,128)(2,1)S(1)} %add_convert_fusion.4), channel_id=1, source_target_pairs={{0,4},{4,0},{1,5},{5,1},{2,6},{6,2},{3,7},{7,3},{8,12},{12,8},{9,1... | collective-permute-start | bytes 1572872 | tf_op jit(solution)/shard_map/ppermute | solution.py:18
  633.4 7.6 %collective-permute-start.66 = (bf16[512,256]{0,1:T(8,128)(2,1)S(1)}, bf16[512,256]{0,1:T(8,128)(2,1)S(1)}, u32[]{:S(2)}, u32[]{:S(2)}) collective-permute-start(bf16[512,256]{0,1:T(8,128)(2,1)S(1)} %get-tuple-element.77), channel_id=1, source_target_pairs={{0,8},{8,0},{16,24},{24,16},{32,40},{40,32},{48,56},{56,48},{64,72... | collective-permute-start | bytes 786440 | tf_op jit(solution)/shard_map/ppermute | solution.py:18
  641.0 8.0 %collective-permute-start.67 = (bf16[512,256]{0,1:T(8,128)(2,1)S(1)}, bf16[512,256]{0,1:T(8,128)(2,1)S(1)}, u32[]{:S(2)}, u32[]{:S(2)}) collective-permute-start(bf16[512,256]{0,1:T(8,128)(2,1)S(1)} %fusion.41), channel_id=1, source_target_pairs={{0,16},{16,0},{8,24},{24,8},{32,48},{48,32},{40,56},{56,40},{64,80... | collective-permute-start | bytes 786440 | tf_op jit(solution)/shard_map/ppermute | solution.py:18
  667.7 25.3 %collective-permute-start.69 = (bf16[2048,256]{0,1:T(8,128)(2,1)S(1)}, bf16[2048,256]{0,1:T(8,128)(2,1)S(1)}, u32[]{:S(2)}, u32[]{:S(2)}) collective-permute-start(bf16[2048,256]{0,1:T(8,128)(2,1)S(1)} %add_convert_fusion.1), channel_id=1, source_target_pairs={{0,2},{2,0},{1,3},{3,1},{4,6},{6,4},{5,7},{7,5},{8,10},{10,8},{9,1... | collective-permute-start | bytes 3145736 | tf_op jit(solution)/shard_map/ppermute | solution.py:18
  693.4 25.9 %collective-permute-start.70 = (bf16[2048,256]{0,1:T(8,128)(2,1)S(1)}, bf16[2048,256]{0,1:T(8,128)(2,1)S(1)}, u32[]{:S(2)}, u32[]{:S(2)}) collective-permute-start(bf16[2048,256]{0,1:T(8,128)(2,1)S(1)} %add_convert_fusion), channel_id=1, source_target_pairs={{0,4},{4,0},{1,5},{5,1},{2,6},{6,2},{3,7},{7,3},{8,12},{12,8},{9,1... | collective-permute-start | bytes 3145736 | tf_op jit(solution)/shard_map/ppermute | solution.py:18
  720.1 6.7 collective-permute-start.71
  728.7 13.7 %all-to-all-start.4 = ((bf16[8,128,256]{2,1,0:T(8,128)(2,1)}), bf16[8,128,256]{2,1,0:T(8,128)(2,1)S(1)}, u32[]{:S(2)}, u32[]{:S(2)}) async-start(bf16[8,128,256]{2,1,0:T(8,128)(2,1)} %copy.66), calls=%async_computation.4 | async-start | bytes 1048576 | tf_op jit(solution)/shard_map/all_to_all | solution.py:169
  (64 other events, 1095.6 us)
Sparse Core Ops, SparseCore 0:
  13.4 28.4 all-gather.5
  115.0 25.4 all-gather.7
  194.9 26.4 all-gather.9
  273.2 26.6 all-gather.11
  355.1 26.6 all-gather.13
where the time goes:
time: 760 us; the launch traced here: 750 us
  waiting for transfers between devices  503 us (66%)
  starting transfers between devices  86.8 us (11%)
  blocking collectives  53.4 us (7%)
  local copies, waits for them, and re-layouts  38.9 us (5%)
  matrix products  26.4 us (3%)
  other arithmetic  25.6 us (3%)
  between operations  15.6 us (2%)
    ppermute x72, waiting for transfers between devices, partner(): return lax.ppermute(block, axis, route)  446 us
    ppermute x72, starting transfers between devices, partner(): return lax.ppermute(block, axis, route)  83.1 us
    all_to_all x4, blocking collectives, per_device(): lax.all_to_all(outgoing, 'front', split_axis=0, concat_axis=0, tiled=True)  53.4 us
    all_gather x5, waiting for transfers between devices, per_device(): lax.all_gather(jnp.stack([carried, sibling]), 'front', axis=1, tiled=True)  51.3 us
  transfers between devices with their start and end apart: 78, of which 77 were waited for; matrix products, arithmetic and copies ran while one was open for 3% of the time, Pallas kernels for 0%

commit v1 on v0

--- a/solution.py
+++ b/solution.py
@@ -105,7 +105,12 @@
         member = position & group_size - 1
         own_child = child_base(leaves, height) + (position >> height - 1)
         sibling = partner(carried, "leaf", height - 1)
-        pair_blocks = lax.all_gather(jnp.stack([carried, sibling]), "front", axis=1, tiled=True)
+        pair_blocks = jnp.concatenate(
+            lax.all_to_all(
+                jnp.stack([jnp.stack([carried, sibling])] * lax.axis_size("front")), "front", 0, 0
+            ),
+            axis=1,
+        )
         pair_lists = jnp.stack(
             [list_row(extend_lists, own_child), list_row(extend_lists, own_child ^ 1)]
         )

time: 760 us -> 724 us (0.953)
  waiting for transfers between devices: 503 us -> 474 us
  starting transfers between devices: 86.8 us -> 107 us
  between operations: 15.6 us -> 2.24 us
    all_gather x5 -> x0, waiting for transfers between devices: 51.3 us -> none  [per_device(): lax.all_gather(jnp.stack([carried, sibling]), 'front', axis=1, tiled=True)]
    all_to_all x0 -> x5, starting transfers between devices: none -> 21.2 us  [per_device(): lax.all_to_all(jnp.stack([jnp.stack([carried, sibling])] * lax.axis_size(...]
    all_to_all x0 -> x5, waiting for transfers between devices: none -> 14.2 us  [per_device(): lax.all_to_all(jnp.stack([jnp.stack([carried, sibling])] * lax.axis_size(...]
  transfers between devices with their start and end apart: 78 -> 78, of which waited for: 77 -> 76; matrix products, arithmetic and copies ran while one was open for 3% -> 2% of each run, Pallas kernels for 0% -> 0%
where the time goes in v1:
time: 724 us; the launch traced here: 715 us
  waiting for transfers between devices  474 us (65%)
  starting transfers between devices  107 us (15%)
  blocking collectives  53.8 us (7%)
  local copies, waits for them, and re-layouts  36.1 us (5%)
  matrix products  23.6 us (3%)
  other arithmetic  18.1 us (3%)
    ppermute x72, waiting for transfers between devices, partner(): return lax.ppermute(block, axis, route)  453 us
    ppermute x72, starting transfers between devices, partner(): return lax.ppermute(block, axis, route)  82.4 us
    all_to_all x4, blocking collectives, per_device(): lax.all_to_all(outgoing, 'front', split_axis=0, concat_axis=0, tiled=True)  53.8 us
    all_to_all x5, starting transfers between devices, per_device(): lax.all_to_all(jnp.stack([jnp.stack([carried, sibling])] * lax.axis_size(...  21.2 us
  transfers between devices with their start and end apart: 78, of which 76 were waited for; matrix products, arithmetic and copies ran while one was open for 2% of the time, Pallas kernels for 0%

profile of v1, /device:TPU:24, one launch (start us, length us, event | category | flops | bytes accessed | tf_op | source)
XLA Modules:
  0.0 714.6 jit_solution(16496262088969836819)
XLA Ops:
  17.5 9.9 %all-to-all-done = bf16[8,2,128,256]{3,2,1,0:T(8,128)(2,1)S(1)} async-done(((bf16[8,2,128,256]{3,2,1,0:T(8,128)(2,1)}), bf16[8,2,128,256]{3,2,1,0:T(8,128)(2,1)S(1)}, u32[]{:S(2)}, u32[]{:S(2)}) %all-to-all-start) | async-done | bytes 1048608 | tf_op jit(solution)/shard_map/all_to_all | solution.py:109
  35.2 24.6 %collective-permute-done.3 = bf16[2048,256]{0,1:T(8,128)(2,1)S(1)} collective-permute-done((bf16[2048,256]{0,1:T(8,128)(2,1)S(1)}, bf16[2048,256]{0,1:T(8,128)(2,1)S(1)}, u32[]{:S(2)}, u32[]{:S(2)}) %collective-permute-start.3) | collective-permute-done | bytes 1048608 | tf_op jit(solution)/shard_map/ppermute | solution.py:18
  61.2 25.0 %collective-permute-done.4 = bf16[2048,256]{0,1:T(8,128)(2,1)S(1)} collective-permute-done((bf16[2048,256]{0,1:T(8,128)(2,1)S(1)}, bf16[2048,256]{0,1:T(8,128)(2,1)S(1)}, u32[]{:S(2)}, u32[]{:S(2)}) %collective-permute-start.4) | collective-permute-done | bytes 1048608 | tf_op jit(solution)/shard_map/ppermute | solution.py:18
  92.7 4.6 collective-permute-done.8
  108.7 5.1 collective-permute-done.6
  125.6 13.4 %collective-permute-done.10 = bf16[1024,256]{0,1:T(8,128)(2,1)S(1)} collective-permute-done((bf16[1024,256]{0,1:T(8,128)(2,1)S(1)}, bf16[1024,256]{0,1:T(8,128)(2,1)S(1)}, u32[]{:S(2)}, u32[]{:S(2)}) %collective-permute-start.10) | collective-permute-done | bytes 524320 | tf_op jit(solution)/shard_map/ppermute | solution.py:18
  140.2 13.7 %collective-permute-done.11 = bf16[1024,256]{0,1:T(8,128)(2,1)S(1)} collective-permute-done((bf16[1024,256]{0,1:T(8,128)(2,1)S(1)}, bf16[1024,256]{0,1:T(8,128)(2,1)S(1)}, u32[]{:S(2)}, u32[]{:S(2)}) %collective-permute-start.11) | collective-permute-done | bytes 524320 | tf_op jit(solution)/shard_map/ppermute | solution.py:18
  181.5 5.5 collective-permute-done.13
  200.5 6.6 collective-permute-done.19
  210.5 5.8 collective-permute-done.20
  217.7 4.5 collective-permute-done.25
  222.3 5.8 collective-permute-done.26
  239.9 4.5 all-to-all-start.3
  248.4 5.4 collective-permute-done.22
  288.8 5.2 collective-permute-done.38
  305.6 7.9 %collective-permute-start.41 = (bf16[128,256]{0,1:T(8,128)(2,1)S(1)}, bf16[128,256]{0,1:T(8,128)(2,1)S(1)}, u32[]{:S(2)}, u32[]{:S(2)}) collective-permute-start(bf16[128,256]{0,1:T(8,128)(2,1)S(1)} %subtract_convert_fusion.8), channel_id=1, source_target_pairs={{0,128},{128,0},{8,136},{136,8},{16,144},{144,16},{24,152},{152,24... | collective-permute-start | bytes 196616 | tf_op jit(solution)/shard_map/ppermute | solution.py:18
  317.0 5.2 all-to-all-start.4
  326.1 5.2 collective-permute-done.33
  341.4 5.6 collective-permute-start.36
  367.4 7.1 collective-permute-done.45
  374.7 7.9 %collective-permute-done.46 = bf16[512,256]{0,1:T(8,128)(2,1)S(1)} collective-permute-done((bf16[512,256]{0,1:T(8,128)(2,1)S(1)}, bf16[512,256]{0,1:T(8,128)(2,1)S(1)}, u32[]{:S(2)}, u32[]{:S(2)}) %collective-permute-start.46) | collective-permute-done | bytes 262176 | tf_op jit(solution)/shard_map/ppermute | solution.py:18
  382.8 8.3 %collective-permute-done.47 = bf16[512,256]{0,1:T(8,128)(2,1)S(1)} collective-permute-done((bf16[512,256]{0,1:T(8,128)(2,1)S(1)}, bf16[512,256]{0,1:T(8,128)(2,1)S(1)}, u32[]{:S(2)}, u32[]{:S(2)}) %collective-permute-start.47) | collective-permute-done | bytes 262176 | tf_op jit(solution)/shard_map/ppermute | solution.py:18
  391.6 15.2 %collective-permute-done.48 = bf16[512,256]{0,1:T(8,128)(2,1)S(1)} collective-permute-done((bf16[512,256]{0,1:T(8,128)(2,1)S(1)}, bf16[512,256]{0,1:T(8,128)(2,1)S(1)}, u32[]{:S(2)}, u32[]{:S(2)}) %collective-permute-start.48) | collective-permute-done | bytes 262176 | tf_op jit(solution)/shard_map/ppermute | solution.py:18
  406.9 5.3 collective-permute-start.49
  412.3 7.8 %collective-permute-done.49 = bf16[512,256]{0,1:T(8,128)(2,1)S(1)} collective-permute-done((bf16[512,256]{0,1:T(8,128)(2,1)S(1)}, bf16[512,256]{0,1:T(8,128)(2,1)S(1)}, u32[]{:S(2)}, u32[]{:S(2)}) %collective-permute-start.49) | collective-permute-done | bytes 262176 | tf_op jit(solution)/shard_map/ppermute | solution.py:18
  423.8 15.3 %all_to_all.50 = bf16[8,128,256]{2,1,0:T(8,128)(2,1)S(1)} all-to-all(bf16[8,128,256]{2,1,0:T(8,128)(2,1)S(1)} %copy.59), channel_id=1, replica_groups=mesh['leaf'=32,'front'=8] {'front'}, dimensions={0} | all-to-all | bytes 1048576 | tf_op jit(solution)/shard_map/all_to_all | solution.py:174
  441.5 5.0 collective-permute-done.51
  447.5 5.6 collective-permute-done.52
  454.4 7.5 %collective-permute-done.53 = bf16[512,256]{0,1:T(8,128)(2,1)S(1)} collective-permute-done((bf16[512,256]{0,1:T(8,128)(2,1)S(1)}, bf16[512,256]{0,1:T(8,128)(2,1)S(1)}, u32[]{:S(2)}, u32[]{:S(2)}) %collective-permute-start.53) | collective-permute-done | bytes 262176 | tf_op jit(solution)/shard_map/ppermute | solution.py:18
  462.1 7.9 %collective-permute-done.54 = bf16[512,256]{0,1:T(8,128)(2,1)S(1)} collective-permute-done((bf16[512,256]{0,1:T(8,128)(2,1)S(1)}, bf16[512,256]{0,1:T(8,128)(2,1)S(1)}, u32[]{:S(2)}, u32[]{:S(2)}) %collective-permute-start.54) | collective-permute-done | bytes 262176 | tf_op jit(solution)/shard_map/ppermute | solution.py:18
  470.6 8.3 %collective-permute-done.55 = bf16[512,256]{0,1:T(8,128)(2,1)S(1)} collective-permute-done((bf16[512,256]{0,1:T(8,128)(2,1)S(1)}, bf16[512,256]{0,1:T(8,128)(2,1)S(1)}, u32[]{:S(2)}, u32[]{:S(2)}) %collective-permute-start.55) | collective-permute-done | bytes 262176 | tf_op jit(solution)/shard_map/ppermute | solution.py:18
  480.5 9.2 %collective-permute-done.56 = bf16[512,256]{0,1:T(8,128)(2,1)} collective-permute-done((bf16[512,256]{0,1:T(8,128)(2,1)}, bf16[512,256]{0,1:T(8,128)(2,1)}, u32[]{:S(2)}, u32[]{:S(2)}) %collective-permute-start.56) | collective-permute-done | bytes 262176 | tf_op jit(solution)/shard_map/ppermute | solution.py:18
  494.6 12.9 %all_to_all.51 = bf16[8,128,256]{2,1,0:T(8,128)(2,1)S(1)} all-to-all(bf16[8,128,256]{2,1,0:T(8,128)(2,1)S(1)} %copy.63), channel_id=1, replica_groups=mesh['leaf'=32,'front'=8] {'front'}, dimensions={0} | all-to-all | bytes 1048576 | tf_op jit(solution)/shard_map/all_to_all | solution.py:174
  510.1 7.8 %collective-permute-done.58 = bf16[512,256]{0,1:T(8,128)(2,1)S(1)} collective-permute-done((bf16[512,256]{0,1:T(8,128)(2,1)S(1)}, bf16[512,256]{0,1:T(8,128)(2,1)S(1)}, u32[]{:S(2)}, u32[]{:S(2)}) %collective-permute-start.58) | collective-permute-done | bytes 262176 | tf_op jit(solution)/shard_map/ppermute | solution.py:18
  519.0 8.1 %collective-permute-done.59 = bf16[512,256]{0,1:T(8,128)(2,1)S(1)} collective-permute-done((bf16[512,256]{0,1:T(8,128)(2,1)S(1)}, bf16[512,256]{0,1:T(8,128)(2,1)S(1)}, u32[]{:S(2)}, u32[]{:S(2)}) %collective-permute-start.59) | collective-permute-done | bytes 262176 | tf_op jit(solution)/shard_map/ppermute | solution.py:18
  528.5 7.5 %collective-permute-done.60 = bf16[512,256]{0,1:T(8,128)(2,1)S(1)} collective-permute-done((bf16[512,256]{0,1:T(8,128)(2,1)S(1)}, bf16[512,256]{0,1:T(8,128)(2,1)S(1)}, u32[]{:S(2)}, u32[]{:S(2)}) %collective-permute-start.60) | collective-permute-done | bytes 262176 | tf_op jit(solution)/shard_map/ppermute | solution.py:18
  536.2 7.9 %collective-permute-done.61 = bf16[512,256]{0,1:T(8,128)(2,1)S(1)} collective-permute-done((bf16[512,256]{0,1:T(8,128)(2,1)S(1)}, bf16[512,256]{0,1:T(8,128)(2,1)S(1)}, u32[]{:S(2)}, u32[]{:S(2)}) %collective-permute-start.61) | collective-permute-done | bytes 262176 | tf_op jit(solution)/shard_map/ppermute | solution.py:18
  545.7 6.6 collective-permute-done.62
  557.0 12.8 %all_to_all.52 = bf16[8,128,256]{2,1,0:T(8,128)(2,1)S(1)} all-to-all(bf16[8,128,256]{2,1,0:T(8,128)(2,1)S(1)} %copy.67), channel_id=1, replica_groups=mesh['leaf'=32,'front'=8] {'front'}, dimensions={0} | all-to-all | bytes 1048576 | tf_op jit(solution)/shard_map/all_to_all | solution.py:174
  573.0 13.4 %collective-permute-done.64 = bf16[1024,256]{0,1:T(8,128)(2,1)S(1)} collective-permute-done((bf16[1024,256]{0,1:T(8,128)(2,1)S(1)}, bf16[1024,256]{0,1:T(8,128)(2,1)S(1)}, u32[]{:S(2)}, u32[]{:S(2)}) %collective-permute-start.64) | collective-permute-done | bytes 524320 | tf_op jit(solution)/shard_map/ppermute | solution.py:18
  587.6 13.7 %collective-permute-done.65 = bf16[1024,256]{0,1:T(8,128)(2,1)S(1)} collective-permute-done((bf16[1024,256]{0,1:T(8,128)(2,1)S(1)}, bf16[1024,256]{0,1:T(8,128)(2,1)S(1)}, u32[]{:S(2)}, u32[]{:S(2)}) %collective-permute-start.65) | collective-permute-done | bytes 524320 | tf_op jit(solution)/shard_map/ppermute | solution.py:18
  603.1 6.6 collective-permute-done.66
  610.8 8.0 %collective-permute-done.67 = bf16[512,256]{0,1:T(8,128)(2,1)S(1)} collective-permute-done((bf16[512,256]{0,1:T(8,128)(2,1)}, bf16[512,256]{0,1:T(8,128)(2,1)S(1)}, u32[]{:S(2)}, u32[]{:S(2)}) %collective-permute-start.67) | collective-permute-done | bytes 262176 | tf_op jit(solution)/shard_map/ppermute | solution.py:18
  622.3 12.9 %all_to_all.53 = bf16[8,128,256]{2,1,0:T(8,128)(2,1)S(1)} all-to-all(bf16[8,128,256]{2,1,0:T(8,128)(2,1)S(1)} %copy.71), channel_id=1, replica_groups=mesh['leaf'=32,'front'=8] {'front'}, dimensions={0} | all-to-all | bytes 1048576 | tf_op jit(solution)/shard_map/all_to_all | solution.py:174
  639.6 24.6 %collective-permute-done.69 = bf16[2048,256]{0,1:T(8,128)(2,1)S(1)} collective-permute-done((bf16[2048,256]{0,1:T(8,128)(2,1)S(1)}, bf16[2048,256]{0,1:T(8,128)(2,1)S(1)}, u32[]{:S(2)}, u32[]{:S(2)}) %collective-permute-start.69) | collective-permute-done | bytes 1048608 | tf_op jit(solution)/shard_map/ppermute | solution.py:18
  665.6 25.0 %collective-permute-done.70 = bf16[2048,256]{0,1:T(8,128)(2,1)S(1)} collective-permute-done((bf16[2048,256]{0,1:T(8,128)(2,1)S(1)}, bf16[2048,256]{0,1:T(8,128)(2,1)S(1)}, u32[]{:S(2)}, u32[]{:S(2)}) %collective-permute-start.70) | collective-permute-done | bytes 1048608 | tf_op jit(solution)/shard_map/ppermute | solution.py:18
  692.8 5.2 collective-permute-done.71
  707.6 6.1 all-to-all-done.9
  (371 shorter events, 259.4 us)
Async XLA Ops:
  7.1 20.2 %all-to-all-start = ((bf16[8,2,128,256]{3,2,1,0:T(8,128)(2,1)}), bf16[8,2,128,256]{3,2,1,0:T(8,128)(2,1)S(1)}, u32[]{:S(2)}, u32[]{:S(2)}) async-start(bf16[8,2,128,256]{3,2,1,0:T(8,128)(2,1)} %stack.54), calls=%async_computation | async-start | bytes 2097152 | tf_op jit(solution)/shard_map/all_to_all | solution.py:109
  11.5 6.0 collective-permute-start
  34.5 25.3 %collective-permute-start.3 = (bf16[2048,256]{0,1:T(8,128)(2,1)S(1)}, bf16[2048,256]{0,1:T(8,128)(2,1)S(1)}, u32[]{:S(2)}, u32[]{:S(2)}) collective-permute-start(bf16[2048,256]{0,1:T(8,128)(2,1)S(1)} %add_convert_fusion.3), channel_id=1, source_target_pairs={{0,2},{2,0},{1,3},{3,1},{4,6},{6,4},{5,7},{7,5},{8,10},{10,8},{9,1... | collective-permute-start | bytes 3145736 | tf_op jit(solution)/shard_map/ppermute | solution.py:18
  60.2 25.9 %collective-permute-start.4 = (bf16[2048,256]{0,1:T(8,128)(2,1)S(1)}, bf16[2048,256]{0,1:T(8,128)(2,1)S(1)}, u32[]{:S(2)}, u32[]{:S(2)}) collective-permute-start(bf16[2048,256]{0,1:T(8,128)(2,1)S(1)} %add_convert_fusion.2), channel_id=1, source_target_pairs={{0,4},{4,0},{1,5},{5,1},{2,6},{6,2},{3,7},{7,3},{8,12},{12,8},{9,1... | collective-permute-start | bytes 3145736 | tf_op jit(solution)/shard_map/ppermute | solution.py:18
  91.4 5.9 collective-permute-start.8
  98.5 19.4 %all-to-all-start.1 = ((bf16[8,2,128,256]{3,2,1,0:T(8,128)(2,1)}), bf16[8,2,128,256]{3,2,1,0:T(8,128)(2,1)S(1)}, u32[]{:S(2)}, u32[]{:S(2)}) async-start(bf16[8,2,128,256]{3,2,1,0:T(8,128)(2,1)} %stack.59), calls=%async_computation.1 | async-start | bytes 2097152 | tf_op jit(solution)/shard_map/all_to_all | solution.py:109
  107.4 6.5 collective-permute-start.6
  125.0 14.1 %collective-permute-start.10 = (bf16[1024,256]{0,1:T(8,128)(2,1)S(1)}, bf16[1024,256]{0,1:T(8,128)(2,1)S(1)}, u32[]{:S(2)}, u32[]{:S(2)}) collective-permute-start(bf16[1024,256]{0,1:T(8,128)(2,1)S(1)} %add_convert_fusion.7), channel_id=1, source_target_pairs={{0,2},{2,0},{1,3},{3,1},{4,6},{6,4},{5,7},{7,5},{8,10},{10,8},{9,1... | collective-permute-start | bytes 1572872 | tf_op jit(solution)/shard_map/ppermute | solution.py:18
  139.2 14.7 %collective-permute-start.11 = (bf16[1024,256]{0,1:T(8,128)(2,1)S(1)}, bf16[1024,256]{0,1:T(8,128)(2,1)S(1)}, u32[]{:S(2)}, u32[]{:S(2)}) collective-permute-start(bf16[1024,256]{0,1:T(8,128)(2,1)S(1)} %add_convert_fusion.6), channel_id=1, source_target_pairs={{0,4},{4,0},{1,5},{5,1},{2,6},{6,2},{3,7},{7,3},{8,12},{12,8},{9,1... | collective-permute-start | bytes 1572872 | tf_op jit(solution)/shard_map/ppermute | solution.py:18
  161.0 6.0 collective-permute-start.16
  173.5 19.4 %all-to-all-start.2 = ((bf16[8,2,128,256]{3,2,1,0:T(8,128)(2,1)}), bf16[8,2,128,256]{3,2,1,0:T(8,128)(2,1)S(1)}, u32[]{:S(2)}, u32[]{:S(2)}) async-start(bf16[8,2,128,256]{3,2,1,0:T(8,128)(2,1)} %stack.64), calls=%async_computation.2 | async-start | bytes 2097152 | tf_op jit(solution)/shard_map/all_to_all | solution.py:109
  181.1 5.9 collective-permute-start.13
  198.7 8.4 %collective-permute-start.19 = (bf16[512,256]{0,1:T(8,128)(2,1)S(1)}, bf16[512,256]{0,1:T(8,128)(2,1)S(1)}, u32[]{:S(2)}, u32[]{:S(2)}) collective-permute-start(bf16[512,256]{0,1:T(8,128)(2,1)S(1)} %add_convert_fusion.11), channel_id=1, source_target_pairs={{0,2},{2,0},{1,3},{3,1},{4,6},{6,4},{5,7},{7,5},{8,10},{10,8},{9,1... | collective-permute-start | bytes 786440 | tf_op jit(solution)/shard_map/ppermute | solution.py:18
  207.2 9.1 %collective-permute-start.20 = (bf16[512,256]{0,1:T(8,128)(2,1)S(1)}, bf16[512,256]{0,1:T(8,128)(2,1)S(1)}, u32[]{:S(2)}, u32[]{:S(2)}) collective-permute-start(bf16[512,256]{0,1:T(8,128)(2,1)S(1)} %add_convert_fusion.10), channel_id=1, source_target_pairs={{0,4},{4,0},{1,5},{5,1},{2,6},{6,2},{3,7},{7,3},{8,12},{12,8},{9,1... | collective-permute-start | bytes 786440 | tf_op jit(solution)/shard_map/ppermute | solution.py:18
  222.2 5.9 collective-permute-start.26
  239.9 24.9 %all-to-all-start.3 = ((bf16[8,2,128,256]{3,2,1,0:T(8,128)(2,1)}), bf16[8,2,128,256]{3,2,1,0:T(8,128)(2,1)S(1)}, u32[]{:S(2)}, u32[]{:S(2)}) async-start(bf16[8,2,128,256]{3,2,1,0:T(8,128)(2,1)} %stack.134), calls=%async_computation.3 | async-start | bytes 2097152 | tf_op jit(solution)/shard_map/all_to_all | solution.py:109
  258.9 5.9 collective-permute-start.24
  270.2 5.9 collective-permute-start.30
  276.1 6.6 collective-permute-start.31
  288.1 5.9 collective-permute-start.38
  299.3 6.2 collective-permute-start.40
  305.6 10.1 %collective-permute-start.41 = (bf16[128,256]{0,1:T(8,128)(2,1)S(1)}, bf16[128,256]{0,1:T(8,128)(2,1)S(1)}, u32[]{:S(2)}, u32[]{:S(2)}) collective-permute-start(bf16[128,256]{0,1:T(8,128)(2,1)S(1)} %subtract_convert_fusion.8), channel_id=1, source_target_pairs={{0,128},{128,0},{8,136},{136,8},{16,144},{144,16},{24,152},{152,24... | collective-permute-start | bytes 196616 | tf_op jit(solution)/shard_map/ppermute | solution.py:18
  317.0 33.4 %all-to-all-start.4 = ((bf16[8,2,128,256]{3,2,1,0:T(8,128)(2,1)}), bf16[8,2,128,256]{3,2,1,0:T(8,128)(2,1)S(1)}, u32[]{:S(2)}, u32[]{:S(2)}) async-start(bf16[8,2,128,256]{3,2,1,0:T(8,128)(2,1)} %stack.139), calls=%async_computation.4 | async-start | bytes 2097152 | tf_op jit(solution)/shard_map/all_to_all | solution.py:109
  335.3 6.0 collective-permute-start.35
  341.4 9.0 %collective-permute-start.36 = (bf16[256,256]{1,0:T(8,128)(2,1)S(1)}, bf16[256,256]{1,0:T(8,128)(2,1)S(1)}, u32[]{:S(2)}, u32[]{:S(2)}) collective-permute-start(bf16[256,256]{1,0:T(8,128)(2,1)S(1)} %get-tuple-element.30), channel_id=1, source_target_pairs={{0,128},{128,0},{8,136},{136,8},{16,144},{144,16},{24,152},{152,24... | collective-permute-start | bytes 393224 | tf_op jit(solution)/shard_map/ppermute | solution.py:18
  366.8 7.7 %collective-permute-start.45 = (bf16[512,256]{0,1:T(8,128)(2,1)S(1)}, bf16[512,256]{0,1:T(8,128)(2,1)S(1)}, u32[]{:S(2)}, u32[]{:S(2)}) collective-permute-start(bf16[512,256]{0,1:T(8,128)(2,1)S(1)} %get-tuple-element.71), channel_id=1, source_target_pairs={{0,8},{8,0},{16,24},{24,16},{32,40},{40,32},{48,56},{56,48},{64,72... | collective-permute-start | bytes 786440 | tf_op jit(solution)/shard_map/ppermute | solution.py:18
  374.6 8.0 %collective-permute-start.46 = (bf16[512,256]{0,1:T(8,128)(2,1)S(1)}, bf16[512,256]{0,1:T(8,128)(2,1)S(1)}, u32[]{:S(2)}, u32[]{:S(2)}) collective-permute-start(bf16[512,256]{0,1:T(8,128)(2,1)S(1)} %fusion.36), channel_id=1, source_target_pairs={{0,16},{16,0},{8,24},{24,8},{32,48},{48,32},{40,56},{56,40},{64,80... | collective-permute-start | bytes 786440 | tf_op jit(solution)/shard_map/ppermute | solution.py:18
  382.7 8.4 %collective-permute-start.47 = (bf16[512,256]{0,1:T(8,128)(2,1)S(1)}, bf16[512,256]{0,1:T(8,128)(2,1)S(1)}, u32[]{:S(2)}, u32[]{:S(2)}) collective-permute-start(bf16[512,256]{0,1:T(8,128)(2,1)S(1)} %get-tuple-element.28), channel_id=1, source_target_pairs={{0,32},{32,0},{8,40},{40,8},{16,48},{48,16},{24,56},{56,24},{64,96... | collective-permute-start | bytes 786440 | tf_op jit(solution)/shard_map/ppermute | solution.py:18
  391.2 15.6 %collective-permute-start.48 = (bf16[512,256]{0,1:T(8,128)(2,1)S(1)}, bf16[512,256]{0,1:T(8,128)(2,1)S(1)}, u32[]{:S(2)}, u32[]{:S(2)}) collective-permute-start(bf16[512,256]{0,1:T(8,128)(2,1)S(1)} %fusion.37), channel_id=1, source_target_pairs={{0,64},{64,0},{8,72},{72,8},{16,80},{80,16},{24,88},{88,24},{32,96... | collective-permute-start | bytes 786440 | tf_op jit(solution)/shard_map/ppermute | solution.py:18
  406.9 13.2 %collective-permute-start.49 = (bf16[512,256]{0,1:T(8,128)(2,1)S(1)}, bf16[512,256]{0,1:T(8,128)(2,1)S(1)}, u32[]{:S(2)}, u32[]{:S(2)}) collective-permute-start(bf16[512,256]{0,1:T(8,128)(2,1)S(1)} %fusion.58), channel_id=1, source_target_pairs={{0,128},{128,0},{8,136},{136,8},{16,144},{144,16},{24,152},{152,24... | collective-permute-start | bytes 786440 | tf_op jit(solution)/shard_map/ppermute | solution.py:18
  446.5 6.6 collective-permute-start.52
  454.3 7.6 %collective-permute-start.53 = (bf16[512,256]{0,1:T(8,128)(2,1)S(1)}, bf16[512,256]{0,1:T(8,128)(2,1)S(1)}, u32[]{:S(2)}, u32[]{:S(2)}) collective-permute-start(bf16[512,256]{0,1:T(8,128)(2,1)S(1)} %get-tuple-element.73), channel_id=1, source_target_pairs={{0,8},{8,0},{16,24},{24,16},{32,40},{40,32},{48,56},{56,48},{64,72... | collective-permute-start | bytes 786440 | tf_op jit(solution)/shard_map/ppermute | solution.py:18
  462.0 8.0 %collective-permute-start.54 = (bf16[512,256]{0,1:T(8,128)(2,1)S(1)}, bf16[512,256]{0,1:T(8,128)(2,1)S(1)}, u32[]{:S(2)}, u32[]{:S(2)}) collective-permute-start(bf16[512,256]{0,1:T(8,128)(2,1)S(1)} %fusion.38), channel_id=1, source_target_pairs={{0,16},{16,0},{8,24},{24,8},{32,48},{48,32},{40,56},{56,40},{64,80... | collective-permute-start | bytes 786440 | tf_op jit(solution)/shard_map/ppermute | solution.py:18
  470.1 8.8 %collective-permute-start.55 = (bf16[512,256]{0,1:T(8,128)(2,1)S(1)}, bf16[512,256]{0,1:T(8,128)(2,1)S(1)}, u32[]{:S(2)}, u32[]{:S(2)}) collective-permute-start(bf16[512,256]{0,1:T(8,128)(2,1)S(1)} %fusion.111), channel_id=1, source_target_pairs={{0,32},{32,0},{8,40},{40,8},{16,48},{48,16},{24,56},{56,24},{64,96... | collective-permute-start | bytes 786440 | tf_op jit(solution)/shard_map/ppermute | solution.py:18
  479.7 10.0 %collective-permute-start.56 = (bf16[512,256]{0,1:T(8,128)(2,1)}, bf16[512,256]{0,1:T(8,128)(2,1)}, u32[]{:S(2)}, u32[]{:S(2)}) collective-permute-start(bf16[512,256]{0,1:T(8,128)(2,1)} %fusion.39), channel_id=1, source_target_pairs={{0,64},{64,0},{8,72},{72,8},{16,80},{80,16},{24,88},{88,24},{32,96... | collective-permute-start | bytes 786440 | tf_op jit(solution)/shard_map/ppermute | solution.py:18
  509.5 8.4 %collective-permute-start.58 = (bf16[512,256]{0,1:T(8,128)(2,1)S(1)}, bf16[512,256]{0,1:T(8,128)(2,1)S(1)}, u32[]{:S(2)}, u32[]{:S(2)}) collective-permute-start(bf16[512,256]{0,1:T(8,128)(2,1)S(1)} %add_convert_fusion.9), channel_id=1, source_target_pairs={{0,2},{2,0},{1,3},{3,1},{4,6},{6,4},{5,7},{7,5},{8,10},{10,8},{9,1... | collective-permute-start | bytes 786440 | tf_op jit(solution)/shard_map/ppermute | solution.py:18
  518.0 9.1 %collective-permute-start.59 = (bf16[512,256]{0,1:T(8,128)(2,1)S(1)}, bf16[512,256]{0,1:T(8,128)(2,1)S(1)}, u32[]{:S(2)}, u32[]{:S(2)}) collective-permute-start(bf16[512,256]{0,1:T(8,128)(2,1)S(1)} %add_convert_fusion.8), channel_id=1, source_target_pairs={{0,4},{4,0},{1,5},{5,1},{2,6},{6,2},{3,7},{7,3},{8,12},{12,8},{9,1... | collective-permute-start | bytes 786440 | tf_op jit(solution)/shard_map/ppermute | solution.py:18
  528.4 7.6 %collective-permute-start.60 = (bf16[512,256]{0,1:T(8,128)(2,1)S(1)}, bf16[512,256]{0,1:T(8,128)(2,1)S(1)}, u32[]{:S(2)}, u32[]{:S(2)}) collective-permute-start(bf16[512,256]{0,1:T(8,128)(2,1)S(1)} %get-tuple-element.75), channel_id=1, source_target_pairs={{0,8},{8,0},{16,24},{24,16},{32,40},{40,32},{48,56},{56,48},{64,72... | collective-permute-start | bytes 786440 | tf_op jit(solution)/shard_map/ppermute | solution.py:18
  536.1 8.0 %collective-permute-start.61 = (bf16[512,256]{0,1:T(8,128)(2,1)S(1)}, bf16[512,256]{0,1:T(8,128)(2,1)S(1)}, u32[]{:S(2)}, u32[]{:S(2)}) collective-permute-start(bf16[512,256]{0,1:T(8,128)(2,1)S(1)} %fusion.40), channel_id=1, source_target_pairs={{0,16},{16,0},{8,24},{24,8},{32,48},{48,32},{40,56},{56,40},{64,80... | collective-permute-start | bytes 786440 | tf_op jit(solution)/shard_map/ppermute | solution.py:18
  545.6 6.7 collective-permute-start.62
  572.3 14.1 %collective-permute-start.64 = (bf16[1024,256]{0,1:T(8,128)(2,1)S(1)}, bf16[1024,256]{0,1:T(8,128)(2,1)S(1)}, u32[]{:S(2)}, u32[]{:S(2)}) collective-permute-start(bf16[1024,256]{0,1:T(8,128)(2,1)S(1)} %add_convert_fusion.5), channel_id=1, source_target_pairs={{0,2},{2,0},{1,3},{3,1},{4,6},{6,4},{5,7},{7,5},{8,10},{10,8},{9,1... | collective-permute-start | bytes 1572872 | tf_op jit(solution)/shard_map/ppermute | solution.py:18
  586.6 14.7 %collective-permute-start.65 = (bf16[1024,256]{0,1:T(8,128)(2,1)S(1)}, bf16[1024,256]{0,1:T(8,128)(2,1)S(1)}, u32[]{:S(2)}, u32[]{:S(2)}) collective-permute-start(bf16[1024,256]{0,1:T(8,128)(2,1)S(1)} %add_convert_fusion.4), channel_id=1, source_target_pairs={{0,4},{4,0},{1,5},{5,1},{2,6},{6,2},{3,7},{7,3},{8,12},{12,8},{9,1... | collective-permute-start | bytes 1572872 | tf_op jit(solution)/shard_map/ppermute | solution.py:18
  603.0 6.7 collective-permute-start.66
  610.5 8.2 %collective-permute-start.67 = (bf16[512,256]{0,1:T(8,128)(2,1)}, bf16[512,256]{0,1:T(8,128)(2,1)S(1)}, u32[]{:S(2)}, u32[]{:S(2)}) collective-permute-start(bf16[512,256]{0,1:T(8,128)(2,1)} %fusion.41), channel_id=1, source_target_pairs={{0,16},{16,0},{8,24},{24,8},{32,48},{48,32},{40,56},{56,40},{64,80... | collective-permute-start | bytes 786440 | tf_op jit(solution)/shard_map/ppermute | solution.py:18
  638.9 25.3 %collective-permute-start.69 = (bf16[2048,256]{0,1:T(8,128)(2,1)S(1)}, bf16[2048,256]{0,1:T(8,128)(2,1)S(1)}, u32[]{:S(2)}, u32[]{:S(2)}) collective-permute-start(bf16[2048,256]{0,1:T(8,128)(2,1)S(1)} %add_convert_fusion.1), channel_id=1, source_target_pairs={{0,2},{2,0},{1,3},{3,1},{4,6},{6,4},{5,7},{7,5},{8,10},{10,8},{9,1... | collective-permute-start | bytes 3145736 | tf_op jit(solution)/shard_map/ppermute | solution.py:18
  664.6 25.9 %collective-permute-start.70 = (bf16[2048,256]{0,1:T(8,128)(2,1)S(1)}, bf16[2048,256]{0,1:T(8,128)(2,1)S(1)}, u32[]{:S(2)}, u32[]{:S(2)}) collective-permute-start(bf16[2048,256]{0,1:T(8,128)(2,1)S(1)} %add_convert_fusion), channel_id=1, source_target_pairs={{0,4},{4,0},{1,5},{5,1},{2,6},{6,2},{3,7},{7,3},{8,12},{12,8},{9,1... | collective-permute-start | bytes 3145736 | tf_op jit(solution)/shard_map/ppermute | solution.py:18
  691.3 6.7 collective-permute-start.71
  700.0 13.7 %all-to-all-start.9 = ((bf16[8,128,256]{2,1,0:T(8,128)(2,1)}), bf16[8,128,256]{2,1,0:T(8,128)(2,1)S(1)}, u32[]{:S(2)}, u32[]{:S(2)}) async-start(bf16[8,128,256]{2,1,0:T(8,128)(2,1)} %copy.75), calls=%async_computation.9 | async-start | bytes 1048576 | tf_op jit(solution)/shard_map/all_to_all | solution.py:174
  (60 other events, 603.9 us)
